TPU v7x, 32 devices: a whole 2x2x4 slice. The times are simulated.
32 devices in a mesh: node: 8 (over y, x, core), local: 4 (over z).
Axes of the slice: x: 2, y: 2, z: 4, core: 2. Of those that a mesh axis runs over, the one named last changes fastest.
Arguments:
- tokens: bfloat16 [4096, 4096], P(('node', 'local')), may hold values from -6 to 6
- grad_out: bfloat16 [4096, 4096], P(('node', 'local')), may hold values from -6 to 6
- router_logits: float32 [4096, 128], P(('node', 'local')), may hold values from -20 to 280
- group_id: int32 [4096], P(('node', 'local')), may hold values from 0 to 15, as said below
- expert_ids: int32 [4096, 2], P(('node', 'local')), may hold values from 0 to 7, as said below
- w_gate: bfloat16 [8, 4096, 1536], P('node', None, 'local'), may hold values from -0.09375 to 0.09375
- w_up: bfloat16 [8, 4096, 1536], P('node', None, 'local'), may hold values from -0.09375 to 0.09375
- w_down: bfloat16 [8, 1536, 4096], P('node', 'local'), may hold values from -0.15625 to 0.15625
Outputs:
- mixed: bfloat16 [4096, 4096], P(('node', 'local'))
- d_tokens: bfloat16 [4096, 4096], P(('node', 'local'))
- d_logits: float32 [4096, 128], P(('node', 'local'))
- grad_gate: bfloat16 [8, 4096, 1536], P('node', None, 'local')
- grad_up: bfloat16 [8, 4096, 1536], P('node', None, 'local')
- grad_down: bfloat16 [8, 1536, 4096], P('node', 'local')
Inputs may be any that keep to these rules, and one draw needn't show every extreme that they name: `group_id`: A token is computed here when its group is below 1. Among the tokens of one device no expert of those groups is named by more than 6 tokens, and one such expert is named by exactly 6 tokens of every device. `expert_ids`: the two numbers of a token differ; both name experts of the token's group.
All inputs are finite; a program needn't handle non-finite values.
Results may differ from a plain program's by a relative error of at most 0.0065.
Values may be sent and summed in bfloat16 or wider, within the bound.
A program may use at most 192 MiB of HBM per device.

v0:
```python
import jax
import jax.numpy as jnp
from jax import lax
from jax.sharding import PartitionSpec as P

GSIZE = 8
CAP = 6


def gate_weights(logits, group_ids, chosen, inside):
    probabilities = jax.nn.softmax(logits, axis=-1)
    columns = jnp.arange(logits.shape[1], dtype=jnp.int32)
    member = ((columns // GSIZE)[None, :] == group_ids[:, None]).astype(logits.dtype)
    group_mass = jnp.sum(probabilities * member, axis=1)
    picked = jnp.sum(
        jnp.where(chosen[:, :, None] == columns[None, None, :], logits[:, None, :], 0.0), axis=2
    )
    pair_share = jax.nn.softmax(picked, axis=-1)
    return jnp.where(inside[:, None], group_mass[:, None] * pair_share, 0.0)


def spread(buffer):
    arrived = lax.all_to_all(buffer, "node", split_axis=0, concat_axis=2, tiled=True)
    arrived = lax.all_gather(arrived, "local", axis=2, tiled=True)
    return arrived[0]


def collect(partial_sums):
    summed = lax.psum_scatter(partial_sums[None], "local", scatter_dimension=2, tiled=True)
    result = lax.all_to_all(
        summed.astype(jnp.bfloat16), "node", split_axis=2, concat_axis=0, tiled=True
    )
    return result.reshape(-1, result.shape[-1])


def body(tokens, grad_out, router_logits, group_id, expert_ids, w_gate, w_up, w_down):
    owned_count = w_gate.shape[0]
    node_count = lax.axis_size("node")
    expert_total = owned_count * node_count
    window_groups = expert_total // GSIZE
    model_width = tokens.shape[1]
    inside = group_id < window_groups
    chosen = group_id[:, None] * GSIZE + expert_ids
    target = jnp.where(inside[:, None], chosen, expert_total)
    expert_range = jnp.arange(expert_total, dtype=jnp.int32)
    onehot = (target[:, :, None] == expert_range[None, None, :]).astype(jnp.int32)
    per_token = jnp.sum(onehot, axis=1)
    earlier = jnp.cumsum(per_token, axis=0) - per_token
    slot_rank = jnp.sum(onehot * earlier[:, None, :], axis=2)
    slot_index = jnp.where(inside[:, None], target * CAP + slot_rank, -1)
    slot_range = jnp.arange(expert_total * CAP, dtype=jnp.int32)
    first_pick = (slot_range[:, None] == slot_index[None, :, 0]).astype(jnp.bfloat16)
    second_pick = (slot_range[:, None] == slot_index[None, :, 1]).astype(jnp.bfloat16)
    mix_weights, pull_back = jax.vjp(
        lambda values: gate_weights(values, group_id, chosen, inside), router_logits
    )
    grad_f32 = grad_out.astype(jnp.float32)
    first_grad = (mix_weights[:, 0:1] * grad_f32).astype(jnp.bfloat16)
    second_grad = (mix_weights[:, 1:2] * grad_f32).astype(jnp.bfloat16)
    send_rows = (
        jnp.dot(first_pick, tokens, preferred_element_type=jnp.float32)
        + jnp.dot(second_pick, tokens, preferred_element_type=jnp.float32)
    ).astype(jnp.bfloat16)
    send_grads = (
        jnp.dot(first_pick, first_grad, preferred_element_type=jnp.float32)
        + jnp.dot(second_pick, second_grad, preferred_element_type=jnp.float32)
    ).astype(jnp.bfloat16)
    buffer_shape = (node_count, owned_count, CAP, model_width)
    rows_in = spread(send_rows.reshape(buffer_shape))
    gate_pre = jnp.einsum("erd,edf->erf", rows_in, w_gate, preferred_element_type=jnp.float32)
    up_pre = jnp.einsum("erd,edf->erf", rows_in, w_up, preferred_element_type=jnp.float32)
    sigmoid_gate = jax.nn.sigmoid(gate_pre)
    activated = gate_pre * sigmoid_gate
    hidden = (activated * up_pre).astype(jnp.bfloat16)
    partial_out = jnp.einsum("erf,efd->erd", hidden, w_down, preferred_element_type=jnp.float32)
    out_flat = collect(partial_out)
    grads_in = spread(send_grads.reshape(buffer_shape))
    grad_hidden = jnp.einsum("erd,efd->erf", grads_in, w_down, preferred_element_type=jnp.float32)
    grad_gate_pre = (
        grad_hidden * up_pre * sigmoid_gate * (1.0 + gate_pre * (1.0 - sigmoid_gate))
    ).astype(jnp.bfloat16)
    grad_up_pre = (grad_hidden * activated).astype(jnp.bfloat16)
    partial_in = jnp.einsum(
        "erf,edf->erd", grad_gate_pre, w_gate, preferred_element_type=jnp.float32
    ) + jnp.einsum("erf,edf->erd", grad_up_pre, w_up, preferred_element_type=jnp.float32)
    back_flat = collect(partial_in)
    grad_gate = jnp.einsum(
        "erd,erf->edf", rows_in, grad_gate_pre, preferred_element_type=jnp.float32
    ).astype(jnp.bfloat16)
    grad_up = jnp.einsum(
        "erd,erf->edf", rows_in, grad_up_pre, preferred_element_type=jnp.float32
    ).astype(jnp.bfloat16)
    grad_down = jnp.einsum(
        "erf,erd->efd", hidden, grads_in, preferred_element_type=jnp.float32
    ).astype(jnp.bfloat16)
    first_out = jnp.einsum("st,sd->td", first_pick, out_flat, preferred_element_type=jnp.float32)
    second_out = jnp.einsum("st,sd->td", second_pick, out_flat, preferred_element_type=jnp.float32)
    first_back = jnp.einsum("st,sd->td", first_pick, back_flat, preferred_element_type=jnp.float32)
    second_back = jnp.einsum(
        "st,sd->td", second_pick, back_flat, preferred_element_type=jnp.float32
    )
    mixed = (mix_weights[:, 0:1] * first_out + mix_weights[:, 1:2] * second_out).astype(
        jnp.bfloat16
    )
    d_tokens = (first_back + second_back).astype(jnp.bfloat16)
    scores = jnp.stack(
        [jnp.sum(grad_f32 * first_out, axis=1), jnp.sum(grad_f32 * second_out, axis=1)], axis=1
    )
    d_logits = pull_back(scores)[0]
    return (mixed, d_tokens, d_logits, grad_gate, grad_up, grad_down)


def solution(mesh):
    return jax.shard_map(
        body,
        mesh=mesh,
        in_specs=(
            P(("node", "local"), None),
            P(("node", "local"), None),
            P(("node", "local"), None),
            P(("node", "local")),
            P(("node", "local"), None),
            P("node", None, "local"),
            P("node", None, "local"),
            P("node", "local", None),
        ),
        out_specs=(
            P(("node", "local"), None),
            P(("node", "local"), None),
            P(("node", "local"), None),
            P("node", None, "local"),
            P("node", None, "local"),
            P("node", "local", None),
        ),
        check_vma=False,
    )
```

profile of v0, /device:TPU:0, one launch (start us, length us, event | category | flops | bytes accessed | tf_op | source)
XLA Modules:
  0.0 320.4 jit_solution(9817088539204725255)
XLA Ops:
  9.9 1.6 fusion.51
  12.7 15.0 %all_to_all.42 = bf16[8,1,6,4096]{3,2,1,0:T(8,128)(2,1)} all-to-all(bf16[8,1,6,4096]{3,2,1,0:T(8,128)(2,1)} %bitcast.93), channel_id=1, replica_groups=mesh['node'=8,'local'=4] {'node'}, dimensions={0} | all-to-all | bytes 786432 | tf_op jit(solution)/shard_map/all_to_all | solution.py:23
  27.7 1.9 all_to_all.13
  29.7 36.8 %all-gather.3.cloned.1.call-done = bf16[1,1,192,4096]{3,2,1,0:T(8,128)(2,1)} async-done(((bf16[1,1,48,4096]{3,2,1,0:T(8,128)(2,1)}), bf16[1,1,192,4096]{3,2,1,0:T(8,128)(2,1)}) %all-gather.3.cloned.1.call-update) | async-done | bytes 1572880 | tf_op jit(solution)/shard_map/all_gather | solution.py:24
  66.5 3.5 %fusion.15 = f32[192,384]{1,0:T(8,128)S(1)} fusion(bf16[1,4096,384]{2,1,0:T(8,128)(2,1)} %param.13, bf16[1,1,192,4096]{3,2,1,0:T(8,128)(2,1)} %all-gather.3.cloned.1.call-done), kind=kOutput, calls=%fused_computation.27 | convolution fusion | flops 603979776 | bytes 5013504 | tf_op jit(solution)/shard_map/erd,edf->erf/dot_general | solution.py:70
  70.3 1.7 multiply_convert_fusion.2
  72.6 2.7 convolution_bitcast_fusion
  76.9 57.9 %reduce-scatter.3.cloned.1.call-done = f32[1,1,48,4096]{3,2,1,0:T(8,128)} async-done(((f32[1,1,192,4096]{3,2,1,0:T(8,128)}), f32[1,1,48,4096]{3,2,1,0:T(8,128)}) %reduce-scatter.3.cloned.1.call-update) | async-done | bytes 786448 | tf_op jit(solution)/shard_map/reduce_scatter | solution.py:29
  135.9 1.7 copy.64
  138.3 4.9 %reduce = bf16[48,4096]{1,0:T(8,128)(2,1)} reduce(bf16[48,1,1,4096]{3,2,1,0:T(2,128)(2,1)} %bitcast.87, bf16[]{:T(256)} %broadcast.90), dimensions={1,2}, to_apply=%bitcast.86.reduce_sub_computation | reduce | bytes 786434
  143.1 2.1 reshape.179
  145.2 4.1 %all-to-all-start.1 = ((bf16[8,2,12288]{2,1,0:T(2,128)(2,1)}), bf16[8,2,12288]{2,1,0:T(2,128)(2,1)}, u32[]{:S(2)}, u32[]{:S(2)}) async-start(bf16[8,2,12288]{2,1,0:T(2,128)(2,1)} %reshape.179), calls=%async_computation.2 | async-start | bytes 786432 | tf_op jit(solution)/shard_map/all_to_all | solution.py:30
  150.7 6.9 %all-to-all-done.1 = bf16[8,2,12288]{2,1,0:T(2,128)(2,1)} async-done(((bf16[8,2,12288]{2,1,0:T(2,128)(2,1)}), bf16[8,2,12288]{2,1,0:T(2,128)(2,1)}, u32[]{:S(2)}, u32[]{:S(2)}) %all-to-all-start.1) | async-done | bytes 393248 | tf_op jit(solution)/shard_map/all_to_all | solution.py:30
  157.6 3.4 %reshape.180 = bf16[48,1,1,4096]{3,2,1,0:T(2,128)(2,1)} reshape(bf16[8,2,12288]{2,1,0:T(2,128)(2,1)} %all-to-all-done.1) | data formatting | bytes 786432
  161.0 2.0 fusion.35
  163.1 2.2 fusion.19
  168.9 1.9 reshape.176
  170.8 13.8 %all_to_all.43 = bf16[8,1,6,4096]{3,2,1,0:T(8,128)(2,1)} all-to-all(bf16[8,1,6,4096]{3,2,1,0:T(8,128)(2,1)} %bitcast.94), channel_id=1, replica_groups=mesh['node'=8,'local'=4] {'node'}, dimensions={0} | all-to-all | bytes 786432 | tf_op jit(solution)/shard_map/all_to_all | solution.py:23
  184.6 1.9 all_to_all.16
  186.8 35.0 %all-gather.5.cloned.1.call-done = bf16[1,1,192,4096]{3,2,1,0:T(8,128)(2,1)} async-done(((bf16[1,1,48,4096]{3,2,1,0:T(8,128)(2,1)}), bf16[1,1,192,4096]{3,2,1,0:T(8,128)(2,1)}) %all-gather.5.cloned.1.call-update) | async-done | bytes 1572880 | tf_op jit(solution)/shard_map/all_gather | solution.py:24
  221.8 2.8 multiply_convert_fusion
  226.6 2.9 fusion
  231.2 3.8 %add_convert_fusion = bf16[128,4096]{1,0:T(8,128)(2,1)} fusion(f32[128,4096]{1,0:T(8,128)} %copy-done.1, f32[128,4096]{1,0:T(8,128)} %get-tuple-element.24, f32[128]{0:T(128)S(1)} %get-tuple-element.19, f32[128]{0:T(128)S(1)} %get-tuple-element.18), kind=kLoop, calls=%fused_computation.33 | loop fusion | flops 2097152 | bytes 5243904 | tf_op jit(solution)/shard_map/convert_element_type | solution.py:102
  234.9 3.0 fusion.1
  237.9 51.1 %reduce-scatter.5.cloned.1.call-done = f32[1,1,48,4096]{3,2,1,0:T(8,128)} async-done(((f32[1,1,192,4096]{3,2,1,0:T(8,128)}), f32[1,1,48,4096]{3,2,1,0:T(8,128)}) %reduce-scatter.5.cloned.1.call-update) | async-done | bytes 786448 | tf_op jit(solution)/shard_map/reduce_scatter | solution.py:29
  290.2 1.7 copy.63
  291.9 4.1 %reduce.1 = bf16[48,4096]{1,0:T(8,128)(2,1)S(1)} reduce(bf16[48,1,1,4096]{3,2,1,0:T(2,128)(2,1)} %bitcast.88, bf16[]{:T(256)} %broadcast.90), dimensions={1,2}, to_apply=%bitcast.85.reduce_sub_computation | reduce | bytes 786434
  297.1 3.7 %all-to-all-start.3 = ((bf16[8,2,12288]{2,1,0:T(2,128)(2,1)}), bf16[8,2,12288]{2,1,0:T(2,128)(2,1)S(1)}, u32[]{:S(2)}, u32[]{:S(2)}) async-start(bf16[8,2,12288]{2,1,0:T(2,128)(2,1)} %reshape.181), calls=%async_computation.5 | async-start | bytes 786432 | tf_op jit(solution)/shard_map/all_to_all | solution.py:30
  300.8 4.3 %fusion.3 = bf16[1,384,4096]{2,1,0:T(8,128)(2,1)} fusion(bf16[192,384]{1,0:T(8,128)(2,1)} %copy-done.13, bf16[1,1,192,4096]{3,2,1,0:T(8,128)(2,1)} %all-gather.5.cloned.1.call-done), kind=kOutput, calls=%fused_computation.7 | convolution fusion | flops 605552640 | bytes 4866048 | tf_op jit(solution)/shard_map/erf,erd->efd/dot_general | solution.py:93
  305.1 3.0 fusion.2
  310.2 1.9 fusion.33
  312.1 1.7 fusion.4
  (101 shorter events, 21.4 us)
Async XLA Ops:
  7.2 65.5 %copy-start = (bf16[1,384,4096]{2,1,0:T(8,128)(2,1)S(1)}, bf16[1,384,4096]{2,1,0:T(8,128)(2,1)}, u32[]{:S(2)}) copy-start(bf16[1,384,4096]{2,1,0:T(8,128)(2,1)} %param.15) | copy-start | bytes 9437188
  7.2 59.3 %all-gather.3.cloned.1.call-start = ((), (), s32[]{:S(2)}) async-start(), calls=%async_computation.6 | async-start | bytes 1966080 | tf_op jit(solution)/shard_map/all_gather | solution.py:24
  9.8 1.7 copy-start.4
  29.7 105.1 %reduce-scatter.3.cloned.1.call-start = ((), (), s32[]{:S(2)}) async-start(), calls=%async_computation.7 | async-start | bytes 3932160 | tf_op jit(solution)/shard_map/reduce_scatter | solution.py:29
  66.5 3.5 %copy-start.6 = (bf16[1,4096,384]{2,1,0:T(8,128)(2,1)S(1)}, bf16[1,4096,384]{2,1,0:T(8,128)(2,1)}, u32[]{:S(2)}) copy-start(bf16[1,4096,384]{2,1,0:T(8,128)(2,1)} %param.14) | copy-start | bytes 9437188
  66.5 3.8 %copy-start.10 = (bf16[1,1,192,4096]{3,2,1,0:T(8,128)(2,1)S(1)}, bf16[1,1,192,4096]{3,2,1,0:T(8,128)(2,1)}, u32[]{:S(2)}) copy-start(bf16[1,1,192,4096]{3,2,1,0:T(8,128)(2,1)} %all-gather.3.cloned.1.call-done) | copy-start | bytes 4718596
  72.0 0.6 copy-start.13
  75.3 0.8 copy-start.9
  76.4 88.9 %copy-start.18 = (f32[128]{0:T(128)}, f32[128]{0:T(128)S(1)}, u32[]{:S(2)}) copy-start(f32[128]{0:T(128)S(1)} %fusion.60) | copy-start | bytes 1540
  145.2 12.4 %all-to-all-start.1 = ((bf16[8,2,12288]{2,1,0:T(2,128)(2,1)}), bf16[8,2,12288]{2,1,0:T(2,128)(2,1)}, u32[]{:S(2)}, u32[]{:S(2)}) async-start(bf16[8,2,12288]{2,1,0:T(2,128)(2,1)} %reshape.179), calls=%async_computation.2 | async-start | bytes 786432 | tf_op jit(solution)/shard_map/all_to_all | solution.py:30
  149.3 72.5 %all-gather.5.cloned.1.call-start = ((), (), s32[]{:S(2)}) async-start(), calls=%async_computation.8 | async-start | bytes 1966080 | tf_op jit(solution)/shard_map/all_gather | solution.py:24
  161.0 2.0 copy-start.3
  161.0 2.0 copy-start.5
  163.0 2.2 copy-start.1
  163.0 2.3 copy-start.20
  163.0 2.2 copy-start.22
  163.1 2.2 copy-start.25
  163.1 3.0 copy-start.26
  186.6 102.5 %reduce-scatter.5.cloned.1.call-start = ((), (), s32[]{:S(2)}) async-start(), calls=%async_computation.9 | async-start | bytes 3932160 | tf_op jit(solution)/shard_map/reduce_scatter | solution.py:29
  221.8 2.8 copy-start.2
  224.6 1.3 copy-start.14
  224.6 1.3 copy-start.16
  224.7 2.0 copy-start.7
  229.6 0.7 copy-start.19
  229.6 0.8 copy-start.21
  229.6 0.8 copy-start.23
  231.2 3.8 %copy-start.11 = (bf16[1,1,192,4096]{3,2,1,0:T(8,128)(2,1)S(1)}, bf16[1,1,192,4096]{3,2,1,0:T(8,128)(2,1)}, u32[]{:S(2)}) copy-start(bf16[1,1,192,4096]{3,2,1,0:T(8,128)(2,1)} %all-gather.3.cloned.1.call-done) | copy-start | bytes 4718596
  231.2 3.8 %copy-start.15 = (bf16[192,384]{1,0:T(8,128)(2,1)S(1)}, bf16[192,384]{1,0:T(8,128)(2,1)}, u32[]{:S(2)}) copy-start(bf16[192,384]{1,0:T(8,128)(2,1)} %copy-done.14) | copy-start | bytes 442372
  297.1 12.0 %all-to-all-start.3 = ((bf16[8,2,12288]{2,1,0:T(2,128)(2,1)}), bf16[8,2,12288]{2,1,0:T(2,128)(2,1)S(1)}, u32[]{:S(2)}, u32[]{:S(2)}) async-start(bf16[8,2,12288]{2,1,0:T(2,128)(2,1)} %reshape.181), calls=%async_computation.5 | async-start | bytes 786432 | tf_op jit(solution)/shard_map/all_to_all | solution.py:30
  300.8 4.3 %copy-start.12 = (bf16[1,1,192,4096]{3,2,1,0:T(8,128)(2,1)S(1)}, bf16[1,1,192,4096]{3,2,1,0:T(8,128)(2,1)}, u32[]{:S(2)}) copy-start(bf16[1,1,192,4096]{3,2,1,0:T(8,128)(2,1)} %all-gather.3.cloned.1.call-done) | copy-start | bytes 4718596
  300.8 4.3 %copy-start.17 = (bf16[192,384]{1,0:T(8,128)(2,1)S(1)}, bf16[192,384]{1,0:T(8,128)(2,1)}, u32[]{:S(2)}) copy-start(bf16[192,384]{1,0:T(8,128)(2,1)} %copy-done.16) | copy-start | bytes 442372
  310.2 1.9 copy-start.8
  (1 other events, 0.6 us)
Sparse Core Ops, SparseCore 0:
  29.8 36.6 all-gather.2
  75.4 59.2 reduce-scatter.2
  186.7 35.0 all-gather.4
  229.7 59.2 reduce-scatter.4
where the time goes:
time: 321 us; the launch traced here: 320 us
  waiting for transfers between devices  189 us (59%)
  matrix products  36.2 us (11%)
  blocking collectives  28.8 us (9%)
  other arithmetic  22.5 us (7%)
  local copies, waits for them, and re-layouts  21.8 us (7%)
  between operations  14.1 us (4%)
  starting transfers between devices  8.09 us (3%)
    reduce_scatter x2, waiting for transfers between devices, collect(): lax.psum_scatter(partial_sums[None], 'local', scatter_dimension=2, tiled=...  109 us
    all_gather x2, waiting for transfers between devices, spread(): arrived = lax.all_gather(arrived, 'local', axis=2, tiled=True)  71.8 us
    all_to_all x2, blocking collectives, spread(): lax.all_to_all(buffer, 'node', split_axis=0, concat_axis=2, tiled=True)  28.8 us
    unnamed x59, local copies, waits for them, and re-layouts  11.5 us
    unnamed x2, other arithmetic  8.97 us
    all_to_all x2, waiting for transfers between devices, collect(): lax.all_to_all(summed.astype(jnp.bfloat16), 'node', split_axis=2, concat_...  7.99 us
    all_to_all x2, starting transfers between devices, collect(): lax.all_to_all(summed.astype(jnp.bfloat16), 'node', split_axis=2, concat_...  7.75 us
  transfers between devices with their start and end apart: 6, of which 6 were waited for; matrix products, arithmetic and copies ran while one was open for 5% of the time, Pallas kernels for 0%

commit v1 on v0

--- a/solution.py
+++ b/solution.py
@@ -5,6 +5,23 @@
 
 GSIZE = 8
 CAP = 6
+
+
+def in_order(tiles, dim):
+    shape = list(tiles.shape[1:])
+    shape[dim] *= tiles.shape[0]
+    return jnp.moveaxis(tiles, 0, dim).reshape(shape)
+
+
+def doubled(x, axis):
+    size, position = (lax.axis_size(axis), lax.axis_index(axis))
+    blocks, distance = (x[None], 1)
+    while distance < size:
+        theirs = lax.ppermute(blocks, axis, [(i, i ^ distance) for i in range(size)])
+        low = position & distance == 0
+        blocks = jnp.concatenate([jnp.where(low, blocks, theirs), jnp.where(low, theirs, blocks)])
+        distance *= 2
+    return blocks
 
 
 def gate_weights(logits, group_ids, chosen, inside):
@@ -21,7 +38,7 @@
 
 def spread(buffer):
     arrived = lax.all_to_all(buffer, "node", split_axis=0, concat_axis=2, tiled=True)
-    arrived = lax.all_gather(arrived, "local", axis=2, tiled=True)
+    arrived = in_order(doubled(arrived, "local"), 2)
     return arrived[0]
 
 

time: 321 us -> 350 us (1.090)
  waiting for transfers between devices: 189 us -> 204 us
  starting transfers between devices: 8.09 us -> 16 us
  other arithmetic: 22.5 us -> 27.5 us
  local copies, waits for them, and re-layouts: 21.8 us -> 26 us
  matrix products: 36.2 us -> 32.1 us
    ppermute x0 -> x4, waiting for transfers between devices: none -> 84.9 us  [doubled(): lax.ppermute(blocks, axis, [(i, i ^ distance) for i in range(size)])]
    all_gather x2 -> x0, waiting for transfers between devices: 71.8 us -> none  [spread(): arrived = lax.all_gather(arrived, 'local', axis=2, tiled=True)]
    ppermute x0 -> x4, starting transfers between devices: none -> 7.95 us  [doubled(): lax.ppermute(blocks, axis, [(i, i ^ distance) for i in range(size)])]
    unnamed x59 -> x69, local copies, waits for them, and re-layouts: 11.5 us -> 16.5 us
    all_to_all x2 -> x0, local copies, waits for them, and re-layouts: 3.84 us -> none  [spread(): lax.all_to_all(buffer, 'node', split_axis=0, concat_axis=2, tiled=True)]
    select_n x0 -> x4, other arithmetic: none -> 3.66 us  [doubled(): jnp.where(low, blocks, theirs)]
  transfers between devices with their start and end apart: 6 -> 8, of which waited for: 6 -> 8; matrix products, arithmetic and copies ran while one was open for 5% -> 5% of each run, Pallas kernels for 0% -> 0%
where the time goes in v1:
time: 350 us; the launch traced here: 349 us
  waiting for transfers between devices  204 us (58%)
  matrix products  32.1 us (9%)
  blocking collectives  28.9 us (8%)
  other arithmetic  27.5 us (8%)
  local copies, waits for them, and re-layouts  26 us (7%)
  starting transfers between devices  16 us (5%)
  between operations  14.5 us (4%)
    reduce_scatter x2, waiting for transfers between devices, collect(): lax.psum_scatter(partial_sums[None], 'local', scatter_dimension=2, tiled=...  111 us
    ppermute x4, waiting for transfers between devices, doubled(): lax.ppermute(blocks, axis, [(i, i ^ distance) for i in range(size)])  84.9 us
    all_to_all x2, blocking collectives, spread(): lax.all_to_all(buffer, 'node', split_axis=0, concat_axis=2, tiled=True)  28.9 us
    unnamed x69, local copies, waits for them, and re-layouts  16.5 us
    unnamed x2, other arithmetic  8.94 us
    ppermute x4, starting transfers between devices, doubled(): lax.ppermute(blocks, axis, [(i, i ^ distance) for i in range(size)])  7.95 us
    all_to_all x2, starting transfers between devices, collect(): lax.all_to_all(summed.astype(jnp.bfloat16), 'node', split_axis=2, concat_...  7.76 us
    all_to_all x2, waiting for transfers between devices, collect(): lax.all_to_all(summed.astype(jnp.bfloat16), 'node', split_axis=2, concat_...  7.73 us
  transfers between devices with their start and end apart: 8, of which 8 were waited for; matrix products, arithmetic and copies ran while one was open for 5% of the time, Pallas kernels for 0%

profile of v1, /device:TPU:0, one launch (start us, length us, event | category | flops | bytes accessed | tf_op | source)
XLA Modules:
  0.0 348.5 jit_solution(10138919710854186527)
XLA Ops:
  12.7 15.0 %all_to_all.16 = bf16[8,1,6,4096]{3,2,1,0:T(8,128)(2,1)} all-to-all(bf16[8,1,6,4096]{3,2,1,0:T(8,128)(2,1)} %bitcast.89), channel_id=1, replica_groups=mesh['node'=8,'local'=4] {'node'}, dimensions={0} | all-to-all | bytes 786432 | tf_op jit(solution)/shard_map/all_to_all | solution.py:40
  28.9 1.9 collective-permute-start
  30.8 8.7 %collective-permute-done = bf16[1,1,1,48,4096]{4,3,2,1,0:T(8,128)(2,1)} collective-permute-done((bf16[1,1,1,48,4096]{4,3,2,1,0:T(8,128)(2,1)S(1)}, bf16[1,1,1,48,4096]{4,3,2,1,0:T(8,128)(2,1)}, u32[]{:S(2)}, u32[]{:S(2)}) %collective-permute-start) | collective-permute-done | bytes 393248 | tf_op jit(solution)/shard_map/ppermute | solution.py:20
  42.4 2.8 collective-permute-start.1
  45.1 33.3 %collective-permute-done.1 = bf16[2,1,1,48,4096]{4,3,2,1,0:T(8,128)(2,1)} collective-permute-done((bf16[2,1,1,48,4096]{4,3,2,1,0:T(8,128)(2,1)}, bf16[2,1,1,48,4096]{4,3,2,1,0:T(8,128)(2,1)}, u32[]{:S(2)}, u32[]{:S(2)}) %collective-permute-start.1) | collective-permute-done | bytes 786464 | tf_op jit(solution)/shard_map/ppermute | solution.py:20
  80.0 2.3 copy-done.2
  84.1 1.7 multiply_convert_fusion.2
  86.5 2.7 convolution_bitcast_fusion
  90.8 59.5 %reduce-scatter.3.cloned.1.call-done = f32[1,1,48,4096]{3,2,1,0:T(8,128)} async-done(((f32[1,1,192,4096]{3,2,1,0:T(8,128)}), f32[1,1,48,4096]{3,2,1,0:T(8,128)}) %reduce-scatter.3.cloned.1.call-update) | async-done | bytes 786448 | tf_op jit(solution)/shard_map/reduce_scatter | solution.py:46
  151.5 1.7 copy.64
  153.8 4.8 %reduce = bf16[48,4096]{1,0:T(8,128)(2,1)} reduce(bf16[48,1,1,4096]{3,2,1,0:T(2,128)(2,1)} %bitcast.83, bf16[]{:T(256)} %broadcast.90), dimensions={1,2}, to_apply=%bitcast.76.reduce_sub_computation | reduce | bytes 786434
  158.6 2.1 reshape.181
  160.7 4.1 %all-to-all-start.1 = ((bf16[8,2,12288]{2,1,0:T(2,128)(2,1)}), bf16[8,2,12288]{2,1,0:T(2,128)(2,1)}, u32[]{:S(2)}, u32[]{:S(2)}) async-start(bf16[8,2,12288]{2,1,0:T(2,128)(2,1)} %reshape.181), calls=%async_computation.2 | async-start | bytes 786432 | tf_op jit(solution)/shard_map/all_to_all | solution.py:47
  166.4 6.7 %all-to-all-done.1 = bf16[8,2,12288]{2,1,0:T(2,128)(2,1)} async-done(((bf16[8,2,12288]{2,1,0:T(2,128)(2,1)}), bf16[8,2,12288]{2,1,0:T(2,128)(2,1)}, u32[]{:S(2)}, u32[]{:S(2)}) %all-to-all-start.1) | async-done | bytes 393248 | tf_op jit(solution)/shard_map/all_to_all | solution.py:47
  173.2 3.4 reshape.182
  176.5 2.0 fusion.29
  178.6 2.2 fusion.19
  184.4 1.9 reshape.178
  186.3 13.8 %all_to_all.17 = bf16[8,1,6,4096]{3,2,1,0:T(8,128)(2,1)} all-to-all(bf16[8,1,6,4096]{3,2,1,0:T(8,128)(2,1)} %bitcast.90), channel_id=1, replica_groups=mesh['node'=8,'local'=4] {'node'}, dimensions={0} | all-to-all | bytes 786432 | tf_op jit(solution)/shard_map/all_to_all | solution.py:40
  200.2 1.9 broadcast_in_dim.97
  203.0 9.6 %collective-permute-done.2 = bf16[1,1,1,48,4096]{4,3,2,1,0:T(8,128)(2,1)S(1)} collective-permute-done((bf16[1,1,1,48,4096]{4,3,2,1,0:T(8,128)(2,1)}, bf16[1,1,1,48,4096]{4,3,2,1,0:T(8,128)(2,1)S(1)}, u32[]{:S(2)}, u32[]{:S(2)}) %collective-permute-start.2) | collective-permute-done | bytes 393248 | tf_op jit(solution)/shard_map/ppermute | solution.py:20
  213.8 2.4 collective-permute-start.3
  216.1 33.3 %collective-permute-done.3 = bf16[2,1,1,48,4096]{4,3,2,1,0:T(8,128)(2,1)S(1)} collective-permute-done((bf16[2,1,1,48,4096]{4,3,2,1,0:T(8,128)(2,1)S(1)}, bf16[2,1,1,48,4096]{4,3,2,1,0:T(8,128)(2,1)S(1)}, u32[]{:S(2)}, u32[]{:S(2)}) %collective-permute-start.3) | collective-permute-done | bytes 786464 | tf_op jit(solution)/shard_map/ppermute | solution.py:20
  254.3 2.9 fusion
  258.8 3.8 %add_convert_fusion = bf16[128,4096]{1,0:T(8,128)(2,1)} fusion(f32[128,4096]{1,0:T(8,128)} %copy-done.1, f32[128,4096]{1,0:T(8,128)} %get-tuple-element.32, f32[128]{0:T(128)S(1)} %get-tuple-element.27, f32[128]{0:T(128)S(1)} %get-tuple-element.26), kind=kLoop, calls=%fused_computation.33 | loop fusion | flops 2097152 | bytes 5243904 | tf_op jit(solution)/shard_map/convert_element_type | solution.py:119
  262.6 3.0 fusion.1
  265.5 51.3 %reduce-scatter.5.cloned.1.call-done = f32[1,1,48,4096]{3,2,1,0:T(8,128)} async-done(((f32[1,1,192,4096]{3,2,1,0:T(8,128)}), f32[1,1,48,4096]{3,2,1,0:T(8,128)}) %reduce-scatter.5.cloned.1.call-update) | async-done | bytes 786448 | tf_op jit(solution)/shard_map/reduce_scatter | solution.py:46
  319.8 4.1 %reduce.1 = bf16[48,4096]{1,0:T(8,128)(2,1)S(1)} reduce(bf16[48,1,1,4096]{3,2,1,0:T(2,128)(2,1)} %bitcast.84, bf16[]{:T(256)} %broadcast.90), dimensions={1,2}, to_apply=%bitcast.75.reduce_sub_computation | reduce | bytes 786434
  325.0 3.7 %all-to-all-start.3 = ((bf16[8,2,12288]{2,1,0:T(2,128)(2,1)}), bf16[8,2,12288]{2,1,0:T(2,128)(2,1)S(1)}, u32[]{:S(2)}, u32[]{:S(2)}) async-start(bf16[8,2,12288]{2,1,0:T(2,128)(2,1)} %reshape.183), calls=%async_computation.5 | async-start | bytes 786432 | tf_op jit(solution)/shard_map/all_to_all | solution.py:47
  328.7 4.3 %fusion.3 = bf16[1,384,4096]{2,1,0:T(8,128)(2,1)} fusion(bf16[192,384]{1,0:T(8,128)(2,1)} %copy-done.17, bf16[192,4096]{1,0:T(8,128)(2,1)} %bitcast.82), kind=kOutput, calls=%fused_computation.7 | convolution fusion | flops 605552640 | bytes 4866048 | tf_op jit(solution)/shard_map/erf,erd->efd/dot_general | solution.py:110
  333.0 3.0 fusion.2
  338.1 1.9 fusion.27
  (121 shorter events, 38.3 us)
Async XLA Ops:
  7.2 79.4 %copy-start = (bf16[1,384,4096]{2,1,0:T(8,128)(2,1)S(1)}, bf16[1,384,4096]{2,1,0:T(8,128)(2,1)}, u32[]{:S(2)}) copy-start(bf16[1,384,4096]{2,1,0:T(8,128)(2,1)} %param.15) | copy-start | bytes 9437188
  7.2 143.1 %reduce-scatter.3.cloned.1.call-start = ((), (), s32[]{:S(2)}) async-start(), calls=%async_computation.6 | async-start | bytes 3932160 | tf_op jit(solution)/shard_map/reduce_scatter | solution.py:46
  9.8 1.7 copy-start.9
  28.9 2.0 copy-start.16
  28.9 10.6 %collective-permute-start = (bf16[1,1,1,48,4096]{4,3,2,1,0:T(8,128)(2,1)S(1)}, bf16[1,1,1,48,4096]{4,3,2,1,0:T(8,128)(2,1)}, u32[]{:S(2)}, u32[]{:S(2)}) collective-permute-start(bf16[1,1,1,48,4096]{4,3,2,1,0:T(8,128)(2,1)S(1)} %broadcast_in_dim.95), channel_id=1, source_target_pairs={{0,1},{1,0},{2,3},{3,2},{4,5},{5,4},{6,7},{7,6},{8,9},{9,8},{10,11... | collective-permute-start | bytes 1179656 | tf_op jit(solution)/shard_map/ppermute | solution.py:20
  42.4 36.1 %collective-permute-start.1 = (bf16[2,1,1,48,4096]{4,3,2,1,0:T(8,128)(2,1)}, bf16[2,1,1,48,4096]{4,3,2,1,0:T(8,128)(2,1)}, u32[]{:S(2)}, u32[]{:S(2)}) collective-permute-start(bf16[2,1,1,48,4096]{4,3,2,1,0:T(8,128)(2,1)} %pad_maximum_fusion.2), channel_id=1, source_target_pairs={{0,2},{1,3},{2,0},{3,1},{4,6},{5,7},{6,4},{7,5},{8,10},{9,11},{10,... | collective-permute-start | bytes 2359304 | tf_op jit(solution)/shard_map/ppermute | solution.py:20
  79.8 2.5 copy-start.2
  79.9 3.3 copy-start.5
  82.2 1.9 copy-start.12
  90.3 90.5 %copy-start.22 = (f32[128]{0:T(128)}, f32[128]{0:T(128)S(1)}, u32[]{:S(2)}) copy-start(f32[128]{0:T(128)S(1)} %fusion.54) | copy-start | bytes 1540
  160.7 12.4 %all-to-all-start.1 = ((bf16[8,2,12288]{2,1,0:T(2,128)(2,1)}), bf16[8,2,12288]{2,1,0:T(2,128)(2,1)}, u32[]{:S(2)}, u32[]{:S(2)}) async-start(bf16[8,2,12288]{2,1,0:T(2,128)(2,1)} %reshape.181), calls=%async_computation.2 | async-start | bytes 786432 | tf_op jit(solution)/shard_map/all_to_all | solution.py:47
  164.8 152.1 %reduce-scatter.5.cloned.1.call-start = ((), (), s32[]{:S(2)}) async-start(), calls=%async_computation.7 | async-start | bytes 3932160 | tf_op jit(solution)/shard_map/reduce_scatter | solution.py:46
  176.5 2.0 copy-start.4
  176.5 2.0 copy-start.11
  178.5 2.2 copy-start.1
  178.6 2.3 copy-start.24
  178.6 2.2 copy-start.26
  178.6 2.2 copy-start.29
  178.6 3.0 copy-start.30
  202.1 10.5 %collective-permute-start.2 = (bf16[1,1,1,48,4096]{4,3,2,1,0:T(8,128)(2,1)}, bf16[1,1,1,48,4096]{4,3,2,1,0:T(8,128)(2,1)S(1)}, u32[]{:S(2)}, u32[]{:S(2)}) collective-permute-start(bf16[1,1,1,48,4096]{4,3,2,1,0:T(8,128)(2,1)} %broadcast_in_dim.97), channel_id=1, source_target_pairs={{0,1},{1,0},{2,3},{3,2},{4,5},{5,4},{6,7},{7,6},{8,9},{9,8},{10,11... | collective-permute-start | bytes 1179656 | tf_op jit(solution)/shard_map/ppermute | solution.py:20
  213.8 35.7 %collective-permute-start.3 = (bf16[2,1,1,48,4096]{4,3,2,1,0:T(8,128)(2,1)S(1)}, bf16[2,1,1,48,4096]{4,3,2,1,0:T(8,128)(2,1)S(1)}, u32[]{:S(2)}, u32[]{:S(2)}) collective-permute-start(bf16[2,1,1,48,4096]{4,3,2,1,0:T(8,128)(2,1)S(1)} %pad_maximum_fusion.3), channel_id=1, source_target_pairs={{0,2},{1,3},{2,0},{3,1},{4,6},{5,7},{6,4},{7,5},{8,10},{9,11},{10,... | collective-permute-start | bytes 2359304 | tf_op jit(solution)/shard_map/ppermute | solution.py:20
  249.7 2.0 copy-start.8
  250.5 1.9 copy-start.3
  251.8 1.9 copy-start.18
  251.8 1.9 copy-start.20
  252.4 1.9 copy-start.13
  258.8 3.8 %copy-start.6 = (bf16[4,1,1,48,4096]{4,3,2,1,0:T(8,128)(2,1)S(1)}, bf16[4,1,1,48,4096]{4,3,2,1,0:T(8,128)(2,1)}, u32[]{:S(2)}) copy-start(bf16[4,1,1,48,4096]{4,3,2,1,0:T(8,128)(2,1)} %copy-done.5) | copy-start | bytes 4718596
  258.8 3.8 %copy-start.19 = (bf16[192,384]{1,0:T(8,128)(2,1)S(1)}, bf16[192,384]{1,0:T(8,128)(2,1)}, u32[]{:S(2)}) copy-start(bf16[192,384]{1,0:T(8,128)(2,1)} %copy-done.18) | copy-start | bytes 442372
  325.0 12.0 %all-to-all-start.3 = ((bf16[8,2,12288]{2,1,0:T(2,128)(2,1)}), bf16[8,2,12288]{2,1,0:T(2,128)(2,1)S(1)}, u32[]{:S(2)}, u32[]{:S(2)}) async-start(bf16[8,2,12288]{2,1,0:T(2,128)(2,1)} %reshape.183), calls=%async_computation.5 | async-start | bytes 786432 | tf_op jit(solution)/shard_map/all_to_all | solution.py:47
  328.7 4.3 %copy-start.7 = (bf16[4,1,1,48,4096]{4,3,2,1,0:T(8,128)(2,1)S(1)}, bf16[4,1,1,48,4096]{4,3,2,1,0:T(8,128)(2,1)}, u32[]{:S(2)}) copy-start(bf16[4,1,1,48,4096]{4,3,2,1,0:T(8,128)(2,1)} %copy-done.5) | copy-start | bytes 4718596
  328.7 4.3 %copy-start.21 = (bf16[192,384]{1,0:T(8,128)(2,1)S(1)}, bf16[192,384]{1,0:T(8,128)(2,1)}, u32[]{:S(2)}) copy-start(bf16[192,384]{1,0:T(8,128)(2,1)} %copy-done.20) | copy-start | bytes 442372
  338.1 1.9 copy-start.14
  (8 other events, 6.1 us)
Sparse Core Ops, SparseCore 0:
  89.4 60.9 reduce-scatter.2
  257.4 59.4 reduce-scatter.4
